TPU v7x, 32 devices: a whole 2x2x4 slice. The times are simulated.
32 devices in a mesh: gz: 8 (over z, x), gy: 4 (over y, core).
Axes of the slice: x: 2, y: 2, z: 4, core: 2. Of those that a mesh axis runs over, the one named last changes fastest.
Arguments:
- fields: float32 [2, 256, 256, 128], P(None, 'gz', 'gy'), may hold values from -7 to 8
- residual: float32 [2, 256, 256, 128], P(None, 'gz', 'gy'), may hold values from -14 to 14
- past_fields: float32 [20, 2, 256, 256, 128], P(None, None, 'gz', 'gy'), may hold values from -7 to 8
- past_residuals: float32 [20, 2, 256, 256, 128], P(None, None, 'gz', 'gy'), may hold values from -14 to 14
Outputs:
- new_fields: float32 [2, 256, 256, 128], P(None, 'gz', 'gy')
- summary: float32 [3], replicated
All inputs are finite; a program needn't handle non-finite values.
Results may differ from a plain program's by a relative error of at most 0.0003.
Values sent between devices are 32-bit elements; how exact they have to be, the bound alone decides.
A program may use at most 192 MiB of HBM per device.

v0:
```python
import math
import jax
import jax.numpy as jnp
from jax import lax
from jax.sharding import PartitionSpec as P

CHI_N = 20.0
RIDGE = 0.01
STEP_LOCAL = 0.1
EXACT = lax.Precision.HIGHEST


def kernel_total(length):
    decay_len = length / 4.0
    offsets = lax.iota(jnp.int32, length).astype(jnp.float32)
    return jnp.sum(jnp.cosh((0.5 * length - offsets) / decay_len))


def kernel_rows(row_first, row_count, col_first, col_count, length):
    decay_len = length / 4.0
    row_index = row_first + lax.iota(jnp.int32, row_count)[:, None]
    col_index = col_first + lax.iota(jnp.int32, col_count)[None, :]
    lag = jnp.mod(row_index - col_index, length).astype(jnp.float32)
    return jnp.cosh((0.5 * length - lag) / decay_len) / kernel_total(length)


def end_moments(first, count, length):
    decay_len = length / 4.0
    place = (first + lax.iota(jnp.int32, count)).astype(jnp.float32) / decay_len
    return jnp.stack([jnp.exp(place), jnp.exp(-place)])


def far_weights(first, count, own_block, blocks, length):
    decay_len = length / 4.0
    place = (first + lax.iota(jnp.int32, count)).astype(jnp.float32) / decay_len
    block_index = lax.iota(jnp.int32, blocks)
    below = block_index < own_block
    above = block_index > own_block
    wide = math.exp(0.5 * length / decay_len)
    rising = jnp.where(below, wide, jnp.where(above, 1.0 / wide, 0.0))
    falling = jnp.where(below, 1.0 / wide, jnp.where(above, wide, 0.0))
    factor = 0.5 / kernel_total(length)
    weight_rising = factor * jnp.exp(-place)[:, None] * rising[None, :]
    weight_falling = factor * jnp.exp(place)[:, None] * falling[None, :]
    return jnp.stack([weight_rising, weight_falling], axis=2).reshape(count, 2 * blocks)


def shards(fields, residual, past_fields, past_residuals):
    history = past_residuals.shape[0]
    species, height_cells, width_cells, line_cells = residual.shape
    height_total = height_cells * lax.axis_size("gz")
    width_total = width_cells * lax.axis_size("gy")
    cell_total = height_total * width_total * line_cells
    flat_residual = residual.reshape(-1)
    past_rows = past_residuals.reshape(history, -1)
    deltas = flat_residual[None, :] - past_rows
    gram_local = jnp.dot(deltas, deltas.T, precision=EXACT, preferred_element_type=jnp.float32)
    intersect_local = jnp.dot(
        deltas, flat_residual, precision=EXACT, preferred_element_type=jnp.float32
    )
    residual_square = jnp.sum(residual * residual)
    field_square = jnp.sum(fields * fields)
    gram_matrix, intersect = lax.psum((gram_local, intersect_local), ("gz", "gy"))
    diagonal_shift = RIDGE * jnp.trace(gram_matrix) / history + 1.0
    system = gram_matrix + diagonal_shift * jnp.eye(history, dtype=jnp.float32)
    factor = jnp.linalg.cholesky(system)
    forward = lax.linalg.triangular_solve(factor, intersect[:, None], left_side=True, lower=True)
    coeffs = lax.linalg.triangular_solve(
        factor, forward, left_side=True, lower=True, transpose_a=True
    )[:, 0]
    remain_weight = 1.0 - jnp.sum(coeffs)
    field_mixed = remain_weight * fields + jnp.dot(
        coeffs,
        past_fields.reshape(history, -1),
        precision=EXACT,
        preferred_element_type=jnp.float32,
    ).reshape(fields.shape)
    residual_mixed = remain_weight * residual + jnp.dot(
        coeffs, past_rows, precision=EXACT, preferred_element_type=jnp.float32
    ).reshape(residual.shape)
    height_first = lax.axis_index("gz") * height_cells
    width_first = lax.axis_index("gy") * width_cells
    moments = jnp.einsum(
        "ab,sbyx->sayx",
        end_moments(height_first, height_cells, height_total),
        residual_mixed,
        precision=EXACT,
    )
    every_end = lax.all_gather(moments, "gz", axis=1, tiled=True)
    near = jnp.einsum(
        "ab,sbyx->sayx",
        kernel_rows(height_first, height_cells, height_first, height_cells, height_total),
        residual_mixed,
        precision=EXACT,
    )
    far = jnp.einsum(
        "ab,sbyx->sayx",
        far_weights(
            height_first, height_cells, lax.axis_index("gz"), lax.axis_size("gz"), height_total
        ),
        every_end,
        precision=EXACT,
    )
    smoothed_half = near + far
    portion = lax.all_gather(smoothed_half, "gy", axis=2, tiled=True)
    kernel = kernel_rows(width_first, width_cells, jnp.int32(0), portion.shape[2], width_total)
    smoothed = jnp.zeros_like(smoothed_half) + jnp.einsum(
        "ab,szbx->szax", kernel, portion, precision=EXACT
    )
    new_fields = field_mixed + STEP_LOCAL * residual_mixed + smoothed
    split_field = new_fields[0] - new_fields[1]
    sum_field = new_fields[0] + new_fields[1]
    energy_local = jnp.sum(split_field * split_field / (4.0 * CHI_N) - 0.5 * sum_field)
    peak_local = jnp.max(jnp.abs(residual_mixed))
    energy_total, residual_total, field_total = lax.psum(
        (energy_local, residual_square, field_square), ("gz", "gy")
    )
    largest = lax.pmax(peak_local, ("gz", "gy"))
    relative = jnp.sqrt(residual_total / (field_total + 1.0))
    summary = jnp.stack([energy_total / cell_total, relative, largest])
    return (new_fields, summary)


def solution(mesh):
    placed = (
        P(None, "gz", "gy", None),
        P(None, "gz", "gy", None),
        P(None, None, "gz", "gy", None),
        P(None, None, "gz", "gy", None),
    )
    return jax.shard_map(
        shards,
        mesh=mesh,
        in_specs=placed,
        out_specs=(P(None, "gz", "gy", None), P()),
        check_vma=False,
    )
```

profile of v0, /device:TPU:0, one launch (start us, length us, event | category | flops | bytes accessed | tf_op | source)
XLA Modules:
  0.0 577.8 jit_solution(16843497883057855397)
XLA Ops:
  7.2 0.0 all-gather.3.cloned.1.call-start
  7.2 32.5 %broadcast_subtract_fusion = f32[20,2,32,64,128]{4,3,2,1,0:T(8,128)} fusion(f32[20,2,32,64,128]{4,3,2,1,0:T(8,128)} %param.7, f32[2,32,64,128]{3,2,1,0:T(8,128)} %param.5), kind=kLoop, calls=%fused_computation.8 | loop fusion | flops 10485760 | bytes 85983232 | tf_op jit(solution)/shard_map/sub | solution.py:56
  39.7 0.0 copy-start
  39.8 110.5 %fusion.21 = f32[20,20]{1,0:T(8,128)S(1)} fusion(f32[20,2,32,64,128]{4,3,2,1,0:T(8,128)} %broadcast_subtract_fusion), kind=kOutput, calls=%fused_computation.22 | convolution fusion | flops 2516582400 | bytes 41944640 | tf_op jit(solution)/shard_map/dot_general | solution.py:57
  150.2 0.0 copy-done
  150.2 75.0 %fusion.24 = f32[20]{0:T(128)S(1)} fusion(f32[2,32,64,128,1]{3,4,2,1,0:T(1,128)S(1)} %bitcast.108, f32[20,2,32,64,128]{4,3,2,1,0:T(8,128)} %broadcast_subtract_fusion), kind=kOutput, calls=%fused_computation.24 | convolution fusion | flops 125829120 | bytes 44040272 | tf_op jit(solution)/shard_map/dot_general | solution.py:58
  225.2 42.1 %all-reduce.1 = (f32[20,20]{1,0:T(8,128)S(1)}, f32[20]{0:T(128)S(1)}) all-reduce(f32[20,20]{1,0:T(8,128)S(1)} %fusion.21, f32[20]{0:T(128)S(1)} %fusion.24), channel_id=1, replica_groups=mesh['gz'=8,'gy'=4] {'gz','gy'}, use_global_device_ids=true, to_apply=%region_0.0 | all-reduce | flops 420 | bytes 3360 | tf_op jit(solution)/shard_map/psum | solution.py:63
  267.4 0.6 select_reduce_fusion.1
  268.6 0.1 copy.14
  268.7 1.8 cholesky.17
  270.6 0.6 compare_reduce_fusion
  271.2 0.6 fusion.69
  271.9 1.5 custom-call.8
  273.4 0.1 convolution_bitcast_fusion
  273.6 0.8 bitcast_reduce_fusion
  275.0 0.0 copy-start.1
  275.0 74.0 %fusion.4 = f32[1,2,32,64,128]{4,0,3,2,1:T(1,128)S(1)} fusion(f32[2,32,64,128,20]{3,2,1,0,4:T(8,128)} %bitcast.106, f32[1,20]{1,0:T(1,128)S(1)} %get-tuple-element.11), kind=kOutput, calls=%fused_computation.4 | convolution fusion | flops 125829120 | bytes 44040272 | tf_op jit(solution)/shard_map/dot_general | solution.py:78
  349.0 0.0 copy-done.1
  349.0 1.3 abs_reduce_fusion
  350.3 2.4 fusion.18
  352.7 0.7 copy.17
  353.3 0.0 all-gather.3.cloned.1.call-update
  353.4 0.0 all-gather.5.cloned.1.call-start
  353.4 0.7 add_reduce_fusion
  354.8 0.1 broadcast_multiply_fusion
  354.9 0.1 broadcast_multiply_fusion.1
  355.0 38.6 %all-gather.3.cloned.1.call-done = f32[2,16,64,128]{3,2,0,1:T(8,128)} async-done(((f32[2,2,64,128]{3,2,0,1:T(8,128)}), f32[2,16,64,128]{3,2,0,1:T(8,128)}) %all-gather.3.cloned.1.call-update) | async-done | bytes 1048592 | tf_op jit(solution)/shard_map/all_gather | solution.py:89
  393.6 3.5 fusion.27
  397.1 5.3 add_bitcast_fusion
  402.5 0.0 all-gather.5.cloned.1.call-update
  402.5 39.2 %pmax.7 = f32[1]{0:T(128)} all-reduce(f32[1]{0:T(128)} %bitcast.37), channel_id=1, replica_groups=mesh['gz'=8,'gy'=4] {'gz','gy'}, use_global_device_ids=true, to_apply=%region_14.15 | all-reduce | flops 1 | bytes 8 | tf_op jit(solution)/shard_map/pmax | solution.py:118
  441.7 2.7 multiply_reduce_fusion
  444.4 63.8 %fusion.6 = f32[1,2,32,64,128]{4,0,3,2,1:T(1,128)} fusion(f32[2,32,64,128,20]{3,2,1,0,4:T(8,128)} %bitcast.107, f32[1,20]{1,0:T(1,128)S(1)} %get-tuple-element.11), kind=kOutput, calls=%fused_computation.6 | convolution fusion | flops 125829120 | bytes 44040272 | tf_op jit(solution)/shard_map/dot_general | solution.py:72
  508.2 0.0 all-gather.5.cloned.1.call-done
  508.2 15.2 %bitcast_add_fusion = f32[2,32,64,128]{3,2,1,0:T(8,128)S(1)} fusion(f32[2,32,64,128]{3,2,1,0:T(8,128)S(1)} %get-tuple-element.8, f32[2,32,64,128]{3,2,1,0:T(8,128)} %bitcast.109, f32[2,32,64,128]{3,2,1,0:T(8,128)} %param.4, f32[2,32,256,128]{3,1,2,0:T(8,128)} %all-gather.5.cloned.1.call-done, f32[]{:T(128)S(6)} %sub.67, f32[]{:T(128)} %add_reduce_fusion, ...), kind=kOutput, calls=%fused_computation.11 | convolution fusion | flops 1613545472 | bytes 16777480 | tf_op jit(solution)/shard_map/ab,szbx->szax/dot_general | solution.py:107
  523.4 0.0 copy-start.2
  523.5 1.3 copy-done.2
  524.8 0.9 subtract_reduce_fusion
  525.7 41.7 %all-reduce = (f32[]{:T(128)}, f32[]{:T(128)}, f32[]{:T(128)}) all-reduce(f32[]{:T(128)} %get-tuple-element.9, f32[]{:T(128)} %multiply_reduce_fusion, f32[]{:T(128)} %subtract_reduce_fusion), channel_id=1, replica_groups=mesh['gz'=8,'gy'=4] {'gz','gy'}, use_global_device_ids=true, to_apply=%region_10.11 | all-reduce | flops 3 | bytes 24 | tf_op jit(solution)/shard_map/psum | solution.py:115
  569.4 1.1 pad_maximum_fusion.1
  (9 shorter events, 0.1 us)
Async XLA Ops:
  7.2 386.5 %all-gather.3.cloned.1.call-start = ((), (), s32[]{:S(2)}) async-start(), calls=%async_computation | async-start | bytes 1179648 | tf_op jit(solution)/shard_map/all_gather | solution.py:89
  39.7 110.5 %copy-start = (f32[2,32,64,128]{3,2,1,0:T(8,128)S(1)}, f32[2,32,64,128]{3,2,1,0:T(8,128)}, u32[]{:S(2)}) copy-start(f32[2,32,64,128]{3,2,1,0:T(8,128)} %param.5) | copy-start | bytes 6291460
  275.0 74.0 %copy-start.1 = (f32[2,32,64,128]{3,2,1,0:T(8,128)S(1)}, f32[2,32,64,128]{3,2,1,0:T(8,128)}, u32[]{:S(2)}) copy-start(f32[2,32,64,128]{3,2,1,0:T(8,128)} %param.5) | copy-start | bytes 6291460
  353.4 154.9 %all-gather.5.cloned.1.call-start = ((), (), s32[]{:S(2)}) async-start(), calls=%async_computation.1 | async-start | bytes 10485760 | tf_op jit(solution)/shard_map/all_gather | solution.py:105
  523.4 1.3 copy-start.2
Sparse Core Ops, SparseCore 0:
  353.5 40.0 all-gather.2
  402.6 57.8 all-gather.4
where the time goes:
time: 588 us; the launch traced here: 578 us
  matrix products  351 us (60%)
  blocking collectives  123 us (21%)
  other arithmetic  44.7 us (8%)
  waiting for transfers between devices  38.7 us (7%)
  between operations  18.6 us (3%)
    dot_general x1, matrix products, shards(): jnp.dot(deltas, deltas.T, precision=EXACT, preferred_element_type=jnp.flo...  110 us
    dot_general x1, matrix products, shards(): jnp.dot(deltas, flat_residual, precision=EXACT, preferred_element_type=jn...  75 us
    dot_general x1, matrix products, shards(): jnp.dot(coeffs, past_rows, precision=EXACT, preferred_element_type=jnp.fl...  74 us
    dot_general x1, matrix products, shards(): jnp.dot(coeffs, past_fields.reshape(history, -1), precision=EXACT, prefer...  63.8 us
    psum x1, blocking collectives, shards(): lax.psum((gram_local, intersect_local), ('gz', 'gy'))  42.1 us
    psum x1, blocking collectives, shards(): lax.psum((energy_local, residual_square, field_square), ('gz', 'gy'))  41.7 us
    pmax x1, blocking collectives, shards(): largest = lax.pmax(peak_local, ('gz', 'gy'))  39.2 us
    all_gather x1, waiting for transfers between devices, shards(): every_end = lax.all_gather(moments, 'gz', axis=1, tiled=True)  38.6 us
  transfers between devices with their start and end apart: 2, of which 1 were waited for; matrix products, arithmetic and copies ran while one was open for 12% of the time, Pallas kernels for 0%

commit v1 on v0

--- a/solution.py
+++ b/solution.py
@@ -113,7 +113,7 @@
     energy_local = jnp.sum(split_field * split_field / (4.0 * CHI_N) - 0.5 * sum_field)
     peak_local = jnp.max(jnp.abs(residual_mixed))
     energy_total, residual_total, field_total = lax.psum(
-        (energy_local, residual_square, field_square), ("gz", "gy")
+        lax.psum((energy_local, residual_square, field_square), "gy"), "gz"
     )
     largest = lax.pmax(peak_local, ("gz", "gy"))
     relative = jnp.sqrt(residual_total / (field_total + 1.0))

time: 588 us -> 574 us (0.976)
  blocking collectives: 123 us -> 109 us
    psum x1 -> x2, blocking collectives: 41.7 us -> 27.6 us  [the longest x1 20.1 us: shards(): lax.psum(lax.psum((energy_local, residual_square, field_square), 'gy'), '...]
where the time goes in v1:
time: 574 us; the launch traced here: 564 us
  matrix products  351 us (61%)
  blocking collectives  109 us (19%)
  other arithmetic  44.8 us (8%)
  waiting for transfers between devices  38.7 us (7%)
  between operations  18.5 us (3%)
    dot_general x1, matrix products, shards(): jnp.dot(deltas, deltas.T, precision=EXACT, preferred_element_type=jnp.flo...  110 us
    dot_general x1, matrix products, shards(): jnp.dot(deltas, flat_residual, precision=EXACT, preferred_element_type=jn...  75 us
    dot_general x1, matrix products, shards(): jnp.dot(coeffs, past_rows, precision=EXACT, preferred_element_type=jnp.fl...  74 us
    dot_general x1, matrix products, shards(): jnp.dot(coeffs, past_fields.reshape(history, -1), precision=EXACT, prefer...  63.8 us
    psum x1, blocking collectives, shards(): lax.psum((gram_local, intersect_local), ('gz', 'gy'))  42.1 us
    pmax x1, blocking collectives, shards(): largest = lax.pmax(peak_local, ('gz', 'gy'))  39.2 us
    all_gather x1, waiting for transfers between devices, shards(): every_end = lax.all_gather(moments, 'gz', axis=1, tiled=True)  38.6 us
    sub x1, other arithmetic, shards(): deltas = flat_residual[None, :] - past_rows  32.5 us
  transfers between devices with their start and end apart: 2, of which 1 were waited for; matrix products, arithmetic and copies ran while one was open for 12% of the time, Pallas kernels for 0%

profile of v1, /device:TPU:0, one launch (start us, length us, event | category | flops | bytes accessed | tf_op | source)
XLA Modules:
  0.0 563.6 jit_solution(5206733930420624960)
XLA Ops:
  7.2 0.0 all-gather.3.cloned.1.call-start
  7.2 32.5 %broadcast_subtract_fusion = f32[20,2,32,64,128]{4,3,2,1,0:T(8,128)} fusion(f32[20,2,32,64,128]{4,3,2,1,0:T(8,128)} %param.7, f32[2,32,64,128]{3,2,1,0:T(8,128)} %param.5), kind=kLoop, calls=%fused_computation.8 | loop fusion | flops 10485760 | bytes 85983232 | tf_op jit(solution)/shard_map/sub | solution.py:56
  39.7 0.0 copy-start
  39.8 110.5 %fusion.21 = f32[20,20]{1,0:T(8,128)S(1)} fusion(f32[20,2,32,64,128]{4,3,2,1,0:T(8,128)} %broadcast_subtract_fusion), kind=kOutput, calls=%fused_computation.22 | convolution fusion | flops 2516582400 | bytes 41944640 | tf_op jit(solution)/shard_map/dot_general | solution.py:57
  150.2 0.0 copy-done
  150.2 75.0 %fusion.24 = f32[20]{0:T(128)S(1)} fusion(f32[2,32,64,128,1]{3,4,2,1,0:T(1,128)S(1)} %bitcast.108, f32[20,2,32,64,128]{4,3,2,1,0:T(8,128)} %broadcast_subtract_fusion), kind=kOutput, calls=%fused_computation.24 | convolution fusion | flops 125829120 | bytes 44040272 | tf_op jit(solution)/shard_map/dot_general | solution.py:58
  225.2 42.1 %all-reduce = (f32[20,20]{1,0:T(8,128)S(1)}, f32[20]{0:T(128)S(1)}) all-reduce(f32[20,20]{1,0:T(8,128)S(1)} %fusion.21, f32[20]{0:T(128)S(1)} %fusion.24), channel_id=1, replica_groups=mesh['gz'=8,'gy'=4] {'gz','gy'}, use_global_device_ids=true, to_apply=%region_0.0 | all-reduce | flops 420 | bytes 3360 | tf_op jit(solution)/shard_map/psum | solution.py:63
  267.4 0.6 select_reduce_fusion.1
  268.7 0.1 copy.14
  268.8 1.8 cholesky.17
  270.6 0.6 compare_reduce_fusion
  271.3 0.6 fusion.69
  271.9 1.5 custom-call.8
  273.4 0.1 convolution_bitcast_fusion
  273.6 0.8 bitcast_reduce_fusion
  275.0 0.0 copy-start.1
  275.0 74.0 %fusion.4 = f32[1,2,32,64,128]{4,0,3,2,1:T(1,128)S(1)} fusion(f32[2,32,64,128,20]{3,2,1,0,4:T(8,128)} %bitcast.106, f32[1,20]{1,0:T(1,128)S(1)} %get-tuple-element.14), kind=kOutput, calls=%fused_computation.4 | convolution fusion | flops 125829120 | bytes 44040272 | tf_op jit(solution)/shard_map/dot_general | solution.py:78
  349.0 0.0 copy-done.1
  349.0 1.2 abs_reduce_fusion
  350.2 2.4 fusion.18
  352.6 0.7 copy.17
  353.3 0.0 all-gather.3.cloned.1.call-update
  353.3 0.0 all-gather.5.cloned.1.call-start
  353.3 0.7 add_reduce_fusion
  354.8 0.1 broadcast_multiply_fusion
  354.8 0.1 broadcast_multiply_fusion.1
  354.9 38.6 %all-gather.3.cloned.1.call-done = f32[2,16,64,128]{3,2,0,1:T(8,128)} async-done(((f32[2,2,64,128]{3,2,0,1:T(8,128)}), f32[2,16,64,128]{3,2,0,1:T(8,128)}) %all-gather.3.cloned.1.call-update) | async-done | bytes 1048592 | tf_op jit(solution)/shard_map/all_gather | solution.py:89
  393.5 3.5 fusion.27
  397.0 5.3 add_bitcast_fusion
  402.4 0.0 all-gather.5.cloned.1.call-update
  402.4 39.2 %pmax.7 = f32[1]{0:T(128)} all-reduce(f32[1]{0:T(128)} %bitcast.37), channel_id=1, replica_groups=mesh['gz'=8,'gy'=4] {'gz','gy'}, use_global_device_ids=true, to_apply=%region_17.18 | all-reduce | flops 1 | bytes 8 | tf_op jit(solution)/shard_map/pmax | solution.py:118
  441.6 2.7 multiply_reduce_fusion
  444.3 63.8 %fusion.6 = f32[1,2,32,64,128]{4,0,3,2,1:T(1,128)} fusion(f32[2,32,64,128,20]{3,2,1,0,4:T(8,128)} %bitcast.107, f32[1,20]{1,0:T(1,128)S(1)} %get-tuple-element.14), kind=kOutput, calls=%fused_computation.6 | convolution fusion | flops 125829120 | bytes 44040272 | tf_op jit(solution)/shard_map/dot_general | solution.py:72
  508.1 0.0 all-gather.5.cloned.1.call-done
  508.2 15.2 %bitcast_add_fusion = f32[2,32,64,128]{3,2,1,0:T(8,128)S(1)} fusion(f32[2,32,64,128]{3,2,1,0:T(8,128)S(1)} %get-tuple-element.11, f32[2,32,64,128]{3,2,1,0:T(8,128)} %bitcast.109, f32[2,32,64,128]{3,2,1,0:T(8,128)} %param.4, f32[2,32,256,128]{3,1,2,0:T(8,128)} %all-gather.5.cloned.1.call-done, f32[]{:T(128)S(6)} %sub.67, f32[]{:T(128)} %add_reduce_fusion, ...), kind=kOutput, calls=%fused_computation.11 | convolution fusion | flops 1613545472 | bytes 16777480 | tf_op jit(solution)/shard_map/ab,szbx->szax/dot_general | solution.py:107
  523.4 0.0 copy-start.2
  523.4 1.3 copy-done.2
  524.7 0.9 subtract_reduce_fusion
  525.6 7.5 %all-reduce.2 = (f32[]{:T(128)}, f32[]{:T(128)}, f32[]{:T(128)}) all-reduce(f32[]{:T(128)} %get-tuple-element.12, f32[]{:T(128)} %multiply_reduce_fusion, f32[]{:T(128)} %subtract_reduce_fusion), channel_id=1, replica_groups=mesh['gz'=8,'gy'=4] {'gy'}, use_global_device_ids=true, to_apply=%region_11.12 | all-reduce | flops 3 | bytes 24 | tf_op jit(solution)/shard_map/psum | solution.py:116
  533.1 20.1 %all-reduce.1 = (f32[]{:T(128)}, f32[]{:T(128)}, f32[]{:T(128)}) all-reduce(f32[]{:T(128)} %get-tuple-element.7, f32[]{:T(128)} %get-tuple-element.8, f32[]{:T(128)} %get-tuple-element.9), channel_id=1, replica_groups=mesh['gz'=8,'gy'=4] {'gz'}, use_global_device_ids=true, to_apply=%region_12.13 | all-reduce | flops 3 | bytes 24 | tf_op jit(solution)/shard_map/psum | solution.py:115
  555.1 1.3 pad_maximum_fusion.1
  (9 shorter events, 0.1 us)
Async XLA Ops:
  7.2 386.4 %all-gather.3.cloned.1.call-start = ((), (), s32[]{:S(2)}) async-start(), calls=%async_computation | async-start | bytes 1179648 | tf_op jit(solution)/shard_map/all_gather | solution.py:89
  39.7 110.5 %copy-start = (f32[2,32,64,128]{3,2,1,0:T(8,128)S(1)}, f32[2,32,64,128]{3,2,1,0:T(8,128)}, u32[]{:S(2)}) copy-start(f32[2,32,64,128]{3,2,1,0:T(8,128)} %param.5) | copy-start | bytes 6291460
  275.0 74.0 %copy-start.1 = (f32[2,32,64,128]{3,2,1,0:T(8,128)S(1)}, f32[2,32,64,128]{3,2,1,0:T(8,128)}, u32[]{:S(2)}) copy-start(f32[2,32,64,128]{3,2,1,0:T(8,128)} %param.5) | copy-start | bytes 6291460
  353.3 154.9 %all-gather.5.cloned.1.call-start = ((), (), s32[]{:S(2)}) async-start(), calls=%async_computation.1 | async-start | bytes 10485760 | tf_op jit(solution)/shard_map/all_gather | solution.py:105
  523.4 1.3 copy-start.2
Sparse Core Ops, SparseCore 0:
  353.4 40.0 all-gather.2
  402.5 57.8 all-gather.4
